TPU v7x, 32 devices: a whole 2x2x4 slice. The times are simulated.
32 devices in a mesh: member: 2 (over x), tx: 4 (over y, core), ty: 4 (over z).
Axes of the slice: x: 2, y: 2, z: 4, core: 2. Of those that a mesh axis runs over, the one named last changes fastest.
Arguments:
- state: float32 [1024, 128, 128], P(('member', 'tx'), 'ty'), parts along dimension 0, may hold values from -6 to 6
- courant: bfloat16 [1024, 128, 128], P(('member', 'tx'), 'ty'), parts along dimension 0, may hold values from -0.3984375 to 0.3984375
- diffusion: float32 [1024, 128], P(('member', 'tx'), 'ty'), parts along dimension 0, may hold values from 0.02 to 0.2
- conv_mask: int32 [1024, 128], P(('member', 'tx'), 'ty'), parts along dimension 0, may hold values from 0 to 1, as said below
- w_in: bfloat16 [128, 1024], replicated, may hold values from -0.5 to 0.5
- w_hidden: bfloat16 [3, 1024, 1024], replicated, may hold values from -0.1875 to 0.1875
- w_out: bfloat16 [1024, 128], replicated, may hold values from -0.1875 to 0.1875
Outputs:
- state_out: float32 [1024, 128, 128], P(('member', 'tx'), 'ty'), parts along dimension 0
There are 2 independent parts, one for each index of `member`. A program takes and returns all parts, laid end to end along the dimension named above; an argument that names none is the same for every part. Nothing has to cross between parts.
Inputs may be any that keep to these rules, and one draw needn't show every extreme that they name: `conv_mask`: A tile is one device's 128 x 32 columns. A tile's used blocks are ceil(its flagged columns / 32); at most 64, reached by some tile; over a member's tiles they sum to exactly 528.
All inputs are finite; a program needn't handle non-finite values.
Results may differ from a plain program's by a relative error of at most 0.00033.
Values may be sent and summed in bfloat16 or wider, within the bound.
A program may use at most 64 MiB of HBM per device.

v0:
```python
import jax
import jax.numpy as jnp
from jax import lax
from jax.sharding import PartitionSpec as P

BLK = 32
NBLK = 64


def padded_2(value, sides, width):
    for axis, dim in sides:
        count, length = (lax.axis_size(axis), value.shape[dim])
        up = [(i, (i + 1) % count) for i in range(count)]
        down = [(j, i) for i, j in up]
        last = lax.slice_in_dim(value, length - width, length, axis=dim)
        leading = lax.slice_in_dim(value, 0, width, axis=dim)
        before = lax.ppermute(last, axis, up)
        after = lax.ppermute(leading, axis, down)
        value = jnp.concatenate([before, value, after], axis=dim)
    return value


def closure(inputs, w_in, w_hidden, w_out):
    hidden = jax.nn.silu(jnp.dot(inputs, w_in, preferred_element_type=jnp.float32)).astype(
        jnp.bfloat16
    )
    for layer_idx in range(w_hidden.shape[0]):
        hidden = jax.nn.silu(
            jnp.dot(hidden, w_hidden[layer_idx], preferred_element_type=jnp.float32)
        ).astype(jnp.bfloat16)
    return jnp.dot(hidden, w_out, preferred_element_type=jnp.float32).astype(jnp.bfloat16)


def local(state, courant, diffusion, conv_mask, w_in, w_hidden, w_out):
    lon_cells, lat_cells, channels = state.shape
    levels = channels // 2
    padded = padded_2(state, (("tx", 0), ("ty", 1)), 1)
    lat_row = lax.axis_index("ty")
    last_row = lax.axis_size("ty") - 1
    lat_pos = jnp.arange(lat_cells + 2)
    pole_rim = (lat_pos == 0) & (lat_row == 0) | (lat_pos == lat_cells + 1) & (lat_row == last_row)
    padded = jnp.where(pole_rim[None, :, None], jnp.float32(0.0), padded)
    center = padded[1:-1, 1:-1]
    east = padded[2:, 1:-1]
    west = padded[:-2, 1:-1]
    north = padded[1:-1, 2:]
    south = padded[1:-1, :-2]
    wind = courant.astype(jnp.float32)
    along_lon = jnp.concatenate([wind[..., :levels], wind[..., :levels]], -1)
    along_lat = jnp.concatenate([wind[..., levels:], wind[..., levels:]], -1)
    laplace = east + west + north + south - 4.0 * center
    advanced = (
        center
        - 0.5 * along_lon * (east - west)
        - 0.5 * along_lat * (north - south)
        + diffusion[..., None] * laplace
    )
    columns = lon_cells * lat_cells
    capacity = NBLK * BLK
    flags = conv_mask.reshape(columns)
    ranks = jnp.cumsum(flags) - 1
    slot_pos = jnp.where(flags == 1, ranks, capacity)
    features = advanced.reshape(columns, channels).astype(jnp.bfloat16)
    packed = jnp.zeros((capacity, channels), jnp.bfloat16).at[slot_pos].set(features, mode="drop")
    packed_tend = closure(packed, w_in, w_hidden, w_out)
    picked = packed_tend[jnp.minimum(slot_pos, capacity - 1)].astype(jnp.float32)
    added = jnp.where(flags[:, None] == 1, picked, jnp.float32(0.0))
    return (advanced.reshape(columns, channels) + added).reshape(lon_cells, lat_cells, channels)


def solution(mesh):
    return jax.shard_map(
        local,
        mesh=mesh,
        in_specs=(
            P(("member", "tx"), "ty", None),
            P(("member", "tx"), "ty", None),
            P(("member", "tx"), "ty"),
            P(("member", "tx"), "ty"),
            P(),
            P(),
            P(),
        ),
        out_specs=P(("member", "tx"), "ty", None),
        check_vma=False,
    )
```

profile of v0, /device:TPU:0, one launch (start us, length us, event | category | flops | bytes accessed | tf_op | source)
XLA Modules:
  0.0 87.1 jit_solution(11177347372183763163)
XLA Ops:
  0.0 0.8 fusion.32
  0.8 2.4 %collective-permute-start.1 = (f32[1,32,128]{2,1,0:T(8,128)S(1)}, f32[1,32,128]{2,1,0:T(8,128)S(1)}, u32[]{:S(2)}, u32[]{:S(2)}) collective-permute-start(f32[1,32,128]{2,1,0:T(8,128)S(1)} %get-tuple-element.9), channel_id=1, source_target_pairs={{4,0},{8,4},{12,8},{0,12},{5,1},{9,5},{13,9},{1,13},{6,2},{10,6},{... | collective-permute-start | bytes 49160 | tf_op jit(solution)/shard_map/ppermute | solution.py:18
  3.2 0.7 broadcast_compare_fusion
  3.9 0.8 copy.29
  4.8 0.1 copy.27
  4.9 0.1 eq.59
  5.1 0.3 reduce-window.9
  5.5 0.1 slice_reduce_fusion
  5.7 4.2 %fusion.33 = (f32[128,32,64]{2,1,0:T(8,128)}, f32[128,32,64]{2,1,0:T(8,128)}) fusion(bf16[128,32,128]{2,1,0:T(8,128)(2,1)} %param.8), kind=kLoop, calls=%fused_computation.47 | loop fusion | bytes 4194304 | tf_op jit(solution)/shard_map/slice | solution.py:49
  10.0 0.1 copy.26
  10.1 0.2 constant_dynamic-update-slice_fusion.1
  10.5 3.7 %collective-permute-start.3 = (f32[130,1,128]{2,0,1:T(8,128)S(1)}, f32[130,1,128]{2,0,1:T(8,128)S(1)}, u32[]{:S(2)}, u32[]{:S(2)}) collective-permute-start(f32[130,1,128]{2,0,1:T(8,128)S(1)} %copy.23), channel_id=1, source_target_pairs={{1,0},{2,1},{3,2},{0,3},{5,4},{6,5},{7,6},{4,7},{9,8},{10,9},{11,1... | collective-permute-start | bytes 199688 | tf_op jit(solution)/shard_map/ppermute | solution.py:18
  14.1 2.6 %collective-permute-done.3 = f32[130,1,128]{2,0,1:T(8,128)S(1)} collective-permute-done((f32[130,1,128]{2,0,1:T(8,128)S(1)}, f32[130,1,128]{2,0,1:T(8,128)S(1)}, u32[]{:S(2)}, u32[]{:S(2)}) %collective-permute-start.3) | collective-permute-done | bytes 66592 | tf_op jit(solution)/shard_map/ppermute | solution.py:18
  16.8 3.6 %collective-permute-done.2 = f32[130,1,128]{2,0,1:T(8,128)S(1)} collective-permute-done((f32[130,1,128]{2,0,1:T(8,128)S(1)}, f32[130,1,128]{2,0,1:T(8,128)S(1)}, u32[]{:S(2)}, u32[]{:S(2)}) %collective-permute-start.2) | collective-permute-done | bytes 66592 | tf_op jit(solution)/shard_map/ppermute | solution.py:17
  20.5 0.4 maximum_select_fusion
  21.0 1.1 %copy-done.1 = f32[128,32,64]{2,1,0:T(8,128)S(1)} copy-done((f32[128,32,64]{2,1,0:T(8,128)S(1)}, f32[128,32,64]{2,1,0:T(8,128)}, u32[]{:S(2)}) %copy-start.1) | copy-done | bytes 1048600
  22.1 0.6 copy-done.2
  22.7 2.8 %fusion.29 = (bf16[128,32,128]{2,1,0:T(8,128)(2,1)S(1)}, f32[128,32,128]{2,1,0:T(8,128)S(1)}) fusion(f32[128,32]{1,0:T(8,128)S(1)} %copy.26, f32[130,34,128]{2,1,0:T(8,128)S(1)} %maximum_select_fusion, f32[128,32,64]{2,1,0:T(8,128)S(1)} %copy-done.2, f32[128,32,64]{2,1,0:T(8,128)S(1)} %copy-done.1), kind=kLoop, calls=%fused_computation.44 | loop fusion | flops 9437184 | bytes 15745024 | tf_op jit(solution)/shard_map/convert_element_type | solution.py:63
  25.5 11.6 %scatter_custom_fusion = bf16[2048,128]{1,0:T(8,128)(2,1)} fusion(s32[4096]{0:T(1024)S(1)} %bitcast.27, bf16[4096,128]{1,0:T(8,128)(2,1)S(1)} %bitcast.24, bf16[]{:T(256)} %constant.11.clone.1), kind=kCustom, calls=%fused_computation.28 | custom fusion | bytes 524290 | tf_op jit(solution)/shard_map/scatter | solution.py:64
  37.1 10.2 %fusion = f32[2048,1024]{1,0:T(8,128)} fusion(bf16[2048,128]{1,0:T(8,128)(2,1)} %scatter_custom_fusion, bf16[128,1024]{1,0:T(8,128)(2,1)S(1)} %copy-done, bf16[3,1024,1024]{2,1,0:T(8,128)(2,1)} %param.12), kind=kOutput, calls=%fused_computation.6 | convolution fusion | flops 4842323968 | bytes 11272192 | tf_op jit(solution)/shard_map/dot_general | solution.py:29
  47.3 15.4 %fusion.2 = f32[2048,1024]{1,0:T(8,128)} fusion(bf16[3,1024,1024]{2,1,0:T(8,128)(2,1)} %param.12, f32[2048,1024]{1,0:T(8,128)} %fusion), kind=kOutput, calls=%fused_computation.8 | convolution fusion | flops 8610906112 | bytes 20971520 | tf_op jit(solution)/shard_map/dot_general | solution.py:29
  62.6 5.7 %fusion.6 = bf16[2048,128]{1,0:T(8,128)(2,1)S(1)} fusion(bf16[1024,128]{1,0:T(8,128)(2,1)S(1)} %copy-done.5, f32[2048,1024]{1,0:T(8,128)} %fusion.2), kind=kOutput, calls=%fused_computation.12 | convolution fusion | flops 547618816 | bytes 9175040 | tf_op jit(solution)/shard_map/dot_general | solution.py:31
  68.4 15.0 %gather_fusion = bf16[4096,128]{1,0:T(8,128)(2,1)} fusion(bf16[2048,128]{1,0:T(8,128)(2,1)S(1)} %fusion.6, s32[4096]{0:T(1024)S(1)} %broadcast_clamp_fusion), kind=kCustom, calls=%fused_computation | custom fusion | bytes 2113536 | tf_op jit(solution)/shard_map/gather | solution.py:66
  83.4 3.7 %fusion.12 = f32[128,32,128]{2,1,0:T(8,128)} fusion(f32[128,32,128]{2,1,0:T(8,128)S(1)} %get-tuple-element.6, bf16[128,32,128]{2,1,0:T(8,128)(2,1)} %bitcast.23, pred[128,32]{1,0:T(8,128)(4,1)S(1)} %copy.27), kind=kLoop, calls=%fused_computation.21 | loop fusion | flops 1572864 | bytes 5246976 | tf_op jit(solution)/shard_map/add | solution.py:68
  (28 shorter events, 0.6 us)
Async XLA Ops:
  0.0 37.1 %copy-start = (bf16[128,1024]{1,0:T(8,128)(2,1)S(1)}, bf16[128,1024]{1,0:T(8,128)(2,1)}, u32[]{:S(2)}) copy-start(bf16[128,1024]{1,0:T(8,128)(2,1)} %param.11) | copy-start | bytes 786436
  0.8 9.5 %collective-permute-start.1 = (f32[1,32,128]{2,1,0:T(8,128)S(1)}, f32[1,32,128]{2,1,0:T(8,128)S(1)}, u32[]{:S(2)}, u32[]{:S(2)}) collective-permute-start(f32[1,32,128]{2,1,0:T(8,128)S(1)} %get-tuple-element.9), channel_id=1, source_target_pairs={{4,0},{8,4},{12,8},{0,12},{5,1},{9,5},{13,9},{1,13},{6,2},{10,6},{... | collective-permute-start | bytes 49160 | tf_op jit(solution)/shard_map/ppermute | solution.py:18
  3.2 6.9 %collective-permute-start = (f32[1,32,128]{2,1,0:T(8,128)S(1)}, f32[1,32,128]{2,1,0:T(8,128)S(1)}, u32[]{:S(2)}, u32[]{:S(2)}) collective-permute-start(f32[1,32,128]{2,1,0:T(8,128)S(1)} %get-tuple-element.10), channel_id=1, source_target_pairs={{0,4},{4,8},{8,12},{12,0},{1,5},{5,9},{9,13},{13,1},{2,6},{6,10},{... | collective-permute-start | bytes 49160 | tf_op jit(solution)/shard_map/ppermute | solution.py:17
  5.7 4.3 %copy-start.4 = (f32[128,32]{0,1:T(8,128)S(1)}, f32[128,32]{0,1:T(8,128)}, u32[]{:S(2)}) copy-start(f32[128,32]{0,1:T(8,128)} %param.9) | copy-start | bytes 49156
  5.7 4.5 %copy-start.3 = (f32[128,32,128]{2,1,0:T(8,128)S(1)}, f32[128,32,128]{2,1,0:T(8,128)}, u32[]{:S(2)}) copy-start(f32[128,32,128]{2,1,0:T(8,128)} %param.7) | copy-start | bytes 6291460
  10.5 6.2 %collective-permute-start.3 = (f32[130,1,128]{2,0,1:T(8,128)S(1)}, f32[130,1,128]{2,0,1:T(8,128)S(1)}, u32[]{:S(2)}, u32[]{:S(2)}) collective-permute-start(f32[130,1,128]{2,0,1:T(8,128)S(1)} %copy.23), channel_id=1, source_target_pairs={{1,0},{2,1},{3,2},{0,3},{5,4},{6,5},{7,6},{4,7},{9,8},{10,9},{11,1... | collective-permute-start | bytes 199688 | tf_op jit(solution)/shard_map/ppermute | solution.py:18
  14.1 6.3 %collective-permute-start.2 = (f32[130,1,128]{2,0,1:T(8,128)S(1)}, f32[130,1,128]{2,0,1:T(8,128)S(1)}, u32[]{:S(2)}, u32[]{:S(2)}) collective-permute-start(f32[130,1,128]{2,0,1:T(8,128)S(1)} %copy.22), channel_id=1, source_target_pairs={{0,1},{1,2},{2,3},{3,0},{4,5},{5,6},{6,7},{7,4},{8,9},{9,10},{10,1... | collective-permute-start | bytes 199688 | tf_op jit(solution)/shard_map/ppermute | solution.py:17
  20.5 1.6 %copy-start.1 = (f32[128,32,64]{2,1,0:T(8,128)S(1)}, f32[128,32,64]{2,1,0:T(8,128)}, u32[]{:S(2)}) copy-start(f32[128,32,64]{2,1,0:T(8,128)} %get-tuple-element.11) | copy-start | bytes 3145732
  20.5 2.2 %copy-start.2 = (f32[128,32,64]{2,1,0:T(8,128)S(1)}, f32[128,32,64]{2,1,0:T(8,128)}, u32[]{:S(2)}) copy-start(f32[128,32,64]{2,1,0:T(8,128)} %get-tuple-element.12) | copy-start | bytes 3145732
  47.3 15.4 %copy-start.5 = (bf16[1024,128]{1,0:T(8,128)(2,1)S(1)}, bf16[1024,128]{1,0:T(8,128)(2,1)}, u32[]{:S(2)}) copy-start(bf16[1024,128]{1,0:T(8,128)(2,1)} %param.13) | copy-start | bytes 786436
where the time goes:
time: 87.5 us; the launch traced here: 87.1 us
  local copies, waits for them, and re-layouts  35.2 us (40%)
  matrix products  31.2 us (36%)
  other arithmetic  8.2 us (9%)
  waiting for transfers between devices  6.2 us (7%)
  starting transfers between devices  6.09 us (7%)
    dot_general x2, matrix products, closure(): jnp.dot(hidden, w_hidden[layer_idx], preferred_element_type=jnp.float32)  25.5 us
    gather x1, local copies, waits for them, and re-layouts, local(): packed_tend[jnp.minimum(slot_pos, capacity - 1)].astype(jnp.float32)  15 us
    scatter x1, local copies, waits for them, and re-layouts, local(): jnp.zeros((capacity, channels), jnp.bfloat16).at[slot_pos]  11.6 us
    ppermute x2, starting transfers between devices, padded_2(): after = lax.ppermute(leading, axis, down)  6.09 us
    dot_general x1, matrix products, closure(): jnp.dot(hidden, w_out, preferred_element_type=jnp.float32)  5.7 us
    slice x1, local copies, waits for them, and re-layouts, local(): along_lon = jnp.concatenate([wind[..., :levels], wind[..., :levels]], -1)  4.25 us
    add x1, other arithmetic, local(): advanced.reshape(columns, channels) + added  3.75 us
    ppermute x2, waiting for transfers between devices, padded_2(): before = lax.ppermute(last, axis, up)  3.64 us
  transfers between devices with their start and end apart: 4, of which 2 were waited for; matrix products, arithmetic and copies ran while one was open for 8% of the time, Pallas kernels for 0%

commit v1 on v0

v1 whole, which is shorter than its diff:
```python
import functools

import jax
import jax.numpy as jnp
from jax import lax
from jax.experimental import pallas as pl
from jax.experimental.pallas import tpu as pltpu
from jax.sharding import PartitionSpec as P

MESH = pl.DeviceIdType.MESH
PAD = 8
GRP = 8
TM = 512


def advance_kernel(ntx, nty, state_hbm, courant_ref, diffusion_ref, adv_ref, tile, lsem, ssem, rsem):
    lon, lat, ch = courant_ref.shape
    ix, iy = lax.axis_index("tx"), lax.axis_index("ty")
    east, west = lax.rem(ix + 1, ntx), lax.rem(ix + ntx - 1, ntx)
    has_n, has_s = iy < nty - 1, iy > 0

    load = pltpu.make_async_copy(state_hbm, tile.at[pl.ds(1, lon), pl.ds(PAD, lat)], lsem)
    load.start()
    barrier = pltpu.get_barrier_semaphore()
    pl.semaphore_signal(barrier, inc=1, device_id={"tx": east}, device_id_type=MESH)
    pl.semaphore_signal(barrier, inc=1, device_id={"tx": west}, device_id_type=MESH)

    @pl.when(has_n)
    def _():
        pl.semaphore_signal(barrier, inc=1, device_id={"ty": iy + 1}, device_id_type=MESH)

    @pl.when(has_s)
    def _():
        pl.semaphore_signal(barrier, inc=1, device_id={"ty": iy - 1}, device_id_type=MESH)

    @pl.when(jnp.logical_not(has_n))
    def _():
        tile[pl.ds(1, lon), pl.ds(PAD + lat, 1), :] = jnp.zeros((lon, 1, ch), jnp.float32)

    @pl.when(jnp.logical_not(has_s))
    def _():
        tile[pl.ds(1, lon), pl.ds(PAD - 1, 1), :] = jnp.zeros((lon, 1, ch), jnp.float32)

    pl.semaphore_wait(barrier, 2 + has_n.astype(jnp.int32) + has_s.astype(jnp.int32))

    def send(src, dst, k, dev):
        return pltpu.make_async_remote_copy(
            src_ref=src, dst_ref=dst, send_sem=ssem.at[k], recv_sem=rsem.at[k],
            device_id=dev, device_id_type=MESH)

    rows, cols = pl.ds(PAD, lat), pl.ds(1, lon)
    to_n = send(state_hbm.at[:, pl.ds(lat - 1, 1)], tile.at[cols, pl.ds(PAD - 1, 1)], 2, {"ty": iy + 1})
    to_s = send(state_hbm.at[:, pl.ds(0, 1)], tile.at[cols, pl.ds(PAD + lat, 1)], 3, {"ty": iy - 1})
    pl.when(has_n)(to_n.start)
    pl.when(has_s)(to_s.start)
    to_e = send(state_hbm.at[pl.ds(lon - 1, 1)], tile.at[pl.ds(0, 1), rows], 0, {"tx": east})
    to_w = send(state_hbm.at[pl.ds(0, 1)], tile.at[pl.ds(lon + 1, 1), rows], 1, {"tx": west})
    to_e.start()
    to_w.start()
    load.wait()
    to_e.wait()
    to_w.wait()

    @pl.when(has_n)
    def _():
        to_n.wait_send()
        to_s.wait_recv()

    @pl.when(has_s)
    def _():
        to_s.wait_send()
        to_n.wait_recv()

    half = ch // 2
    lane = lax.broadcasted_iota(jnp.int32, (GRP * lat, ch), 1)
    eye = (lax.broadcasted_iota(jnp.int32, (GRP, lat, lat), 1)
           == lax.broadcasted_iota(jnp.int32, (GRP, lat, lat), 2))

    @pl.loop(0, lon // GRP)
    def _(c):
        i0 = pl.multiple_of(c * GRP, GRP)

        def get(di, dj):
            return tile[pl.ds(i0 + 1 + di, GRP), pl.ds(PAD + dj, lat), :].reshape(GRP * lat, ch)

        mid, e, w, n, s = get(0, 0), get(1, 0), get(-1, 0), get(0, 1), get(0, -1)
        wind = courant_ref[pl.ds(i0, GRP)].reshape(GRP * lat, ch).astype(jnp.float32)
        turned = pltpu.roll(wind, half, 1)
        cx = jnp.where(lane < half, wind, turned)
        cy = jnp.where(lane < half, turned, wind)
        d8 = diffusion_ref[pl.ds(i0, GRP), :]
        dif = jnp.sum(jnp.where(eye, d8[:, None, :], 0.0), axis=-1, keepdims=True).reshape(GRP * lat, 1)
        laplace = e + w + n + s - 4.0 * mid
        adv_ref[pl.ds(pl.multiple_of(c * GRP * lat, GRP * lat), GRP * lat), :] = (
            mid - 0.5 * cx * (e - w) - 0.5 * cy * (n - s) + dif * laplace)


def closure_kernel(mask_ref, adv_hbm, win_hbm, whid_hbm, wout_hbm, out_hbm,
                   adv, win, whid, wout, packed, ha, hb, place, base_v, base_s, sems, osem):
    lon, lat = mask_ref.shape
    cols, ch = adv.shape
    wide = GRP * lat
    chunks = cols // wide
    span = wide + 16
    layers = whid.shape[0]
    cp_adv = pltpu.make_async_copy(adv_hbm, adv, sems.at[0])
    cp_in = pltpu.make_async_copy(win_hbm, win, sems.at[1])
    cp_out = pltpu.make_async_copy(wout_hbm, wout, sems.at[2])
    cp_hid = [pltpu.make_async_copy(whid_hbm.at[l], whid.at[l], sems.at[3 + l]) for l in range(layers)]
    cp_adv.start()
    cp_in.start()
    for cp in cp_hid:
        cp.start()
    cp_out.start()

    flags = mask_ref[...].astype(jnp.float32).astype(jnp.bfloat16)
    spread = (lax.broadcasted_iota(jnp.int32, (lat, wide), 1) % lat
              == lax.broadcasted_iota(jnp.int32, (lat, wide), 0)).astype(jnp.float32).astype(jnp.bfloat16)
    rep = jnp.dot(flags, spread, preferred_element_type=jnp.float32)
    keep = (lax.broadcasted_iota(jnp.int32, (lon, wide), 1) // lat
            == lax.broadcasted_iota(jnp.int32, (lon, wide), 0) % GRP)
    rows = jnp.sum(jnp.where(keep, rep, 0.0).reshape(chunks, GRP, wide), axis=1)
    upper = (lax.broadcasted_iota(jnp.int32, (wide, wide), 0)
             < lax.broadcasted_iota(jnp.int32, (wide, wide), 1)).astype(jnp.float32).astype(jnp.bfloat16)
    rank = jnp.dot(rows.astype(jnp.bfloat16), upper, preferred_element_type=jnp.float32)
    total = jnp.sum(rows, axis=1, keepdims=True)
    lower = (lax.broadcasted_iota(jnp.int32, (chunks, chunks), 1)
             < lax.broadcasted_iota(jnp.int32, (chunks, chunks), 0)).astype(jnp.float32).astype(jnp.bfloat16)
    base = jnp.dot(lower, jnp.broadcast_to(total, (chunks, 128)).astype(jnp.bfloat16),
                   preferred_element_type=jnp.float32)
    base_i = base.astype(jnp.int32)
    base_v[...] = base_i
    cp_base = pltpu.make_async_copy(base_v, base_s, sems.at[3 + layers])
    cp_base.start()
    rest = (base_i - (base_i // 16) * 16)[:, :1].astype(jnp.float32)
    place[...] = jnp.where(rows > 0.5, rank + rest, -1.0)
    packed[...] = jnp.zeros_like(packed)
    cp_base.wait()
    cp_adv.wait()

    sub = lax.broadcasted_iota(jnp.int32, (span, wide), 0).astype(jnp.float32)

    def onehot(c):
        row = place[pl.ds(c, 1), :]
        return jnp.where(sub == row, 1.0, 0.0).astype(jnp.bfloat16)

    def start_of(c):
        return pl.multiple_of((base_s[c, 0] // 16) * 16, 16)

    for c in range(chunks):
        b = start_of(c)
        feats = adv[pl.ds(c * wide, wide), :].astype(jnp.bfloat16)
        res = jnp.dot(onehot(c), feats, preferred_element_type=jnp.float32).astype(jnp.bfloat16)
        packed[pl.ds(b, 16), :] = packed[pl.ds(b, 16), :] + res[:16]
        packed[pl.ds(pl.multiple_of(b + 16, 16), wide), :] = res[16:]

    cp_in.wait()
    for cp in cp_hid:
        cp.wait()
    cp_out.wait()

    def silu(v):
        hv = 0.5 * v
        return (hv + hv * jnp.tanh(hv)).astype(jnp.bfloat16)

    hid = win.shape[1]
    step = 256

    @pl.loop(0, cols // 2 // TM)
    def _(t):
        r = pl.ds(pl.multiple_of(t * TM, TM), TM)
        x = packed[r, :]
        for n in range(0, hid, step):
            ha[:, n:n + step] = silu(jnp.dot(x, win[:, n:n + step], preferred_element_type=jnp.float32))
        src, dst = ha, hb
        for l in range(layers):
            for n in range(0, hid, step):
                dst[:, n:n + step] = silu(
                    jnp.dot(src[...], whid[l, :, n:n + step], preferred_element_type=jnp.float32))
            src, dst = dst, src
        packed[r, :] = jnp.dot(src[...], wout[...], preferred_element_type=jnp.float32).astype(jnp.bfloat16)

    outs = []
    for c in range(chunks):
        b = start_of(c)
        got = lax.dot_general(onehot(c), packed[pl.ds(b, span), :], (((0,), (0,)), ((), ())),
                              preferred_element_type=jnp.float32)
        r = pl.ds(c * wide, wide)
        adv[r, :] = adv[r, :] + got
        cp = pltpu.make_async_copy(adv.at[r, :], out_hbm.at[r, :], osem.at[c])
        cp.start()
        outs.append(cp)
    for cp in outs:
        cp.wait()


def local(ntx, nty, state, courant, diffusion, conv_mask, w_in, w_hidden, w_out):
    lon, lat, ch = state.shape
    cols = lon * lat
    hid = w_in.shape[1]
    layers = w_hidden.shape[0]
    wide = GRP * lat
    chunks = cols // wide
    vmem = pl.BlockSpec(memory_space=pltpu.VMEM)
    hbm = pl.BlockSpec(memory_space=pl.ANY)
    adv = pl.pallas_call(
        functools.partial(advance_kernel, ntx, nty),
        out_shape=jax.ShapeDtypeStruct((cols, ch), jnp.float32),
        in_specs=[hbm, vmem, vmem],
        out_specs=vmem,
        scratch_shapes=[
            pltpu.VMEM((lon + 2, lat + 2 * PAD, ch), jnp.float32),
            pltpu.SemaphoreType.DMA,
            pltpu.SemaphoreType.DMA((4,)),
            pltpu.SemaphoreType.DMA((4,)),
        ],
        compiler_params=pltpu.CompilerParams(collective_id=0, has_side_effects=True,
                                             vmem_limit_bytes=16 << 20),
        name="advance",
    )(state, courant, diffusion)
    out = pl.pallas_call(
        closure_kernel,
        out_shape=jax.ShapeDtypeStruct((cols, ch), jnp.float32),
        in_specs=[vmem, hbm, hbm, hbm, hbm],
        out_specs=hbm,
        scratch_shapes=[
            pltpu.VMEM((cols, ch), jnp.float32),
            pltpu.VMEM(w_in.shape, jnp.bfloat16),
            pltpu.VMEM(w_hidden.shape, jnp.bfloat16),
            pltpu.VMEM(w_out.shape, jnp.bfloat16),
            pltpu.VMEM((cols // 2 + wide + 32, ch), jnp.bfloat16),
            pltpu.VMEM((TM, hid), jnp.bfloat16),
            pltpu.VMEM((TM, hid), jnp.bfloat16),
            pltpu.VMEM((chunks, wide), jnp.float32),
            pltpu.VMEM((chunks, 128), jnp.int32),
            pltpu.SMEM((chunks, 128), jnp.int32),
            pltpu.SemaphoreType.DMA((4 + layers,)),
            pltpu.SemaphoreType.DMA((chunks,)),
        ],
        compiler_params=pltpu.CompilerParams(vmem_limit_bytes=40 << 20),
        name="closure",
    )(conv_mask, adv, w_in, w_hidden, w_out)
    return out.reshape(lon, lat, ch)


def solution(mesh):
    spec = P(("member", "tx"), "ty", None)
    flat = P(("member", "tx"), "ty")
    return jax.shard_map(
        functools.partial(local, mesh.shape["tx"], mesh.shape["ty"]),
        mesh=mesh,
        in_specs=(spec, spec, flat, flat, P(), P(), P()),
        out_specs=spec,
        check_vma=False,
    )
```

time: 87.5 us -> 38.4 us (0.44)
  matrix products: 31.2 us -> 0 us
  Pallas kernels: 0 us -> 30.8 us
  local copies, waits for them, and re-layouts: 35.2 us -> 7.23 us
  other arithmetic: 8.2 us -> 0 us
  waiting for transfers between devices: 6.2 us -> 0 us
  starting transfers between devices: 6.09 us -> 0 us
    dot_general x3 -> x0, matrix products: 31.2 us -> none  [the longest x2 25.5 us: closure(): jnp.dot(hidden, w_hidden[layer_idx], preferred_element_type=jnp.float32)]
    pallas_call x0 -> x2, Pallas kernels: none -> 30.8 us  [the longest x1 21 us: local(): pl.pallas_call(closure_kernel, out_shape=jax.ShapeDtypeStruct((cols, ch),...]
    gather x1 -> x0, local copies, waits for them, and re-layouts: 15 us -> none  [local(): packed_tend[jnp.minimum(slot_pos, capacity - 1)].astype(jnp.float32)]
    scatter x1 -> x0, local copies, waits for them, and re-layouts: 11.6 us -> none  [local(): jnp.zeros((capacity, channels), jnp.bfloat16).at[slot_pos]]
    ppermute x4 -> x0, waiting for transfers between devices: 6.2 us -> none  [the longest x2 3.64 us: padded_2(): before = lax.ppermute(last, axis, up)]
    ppermute x4 -> x0, starting transfers between devices: 6.09 us -> none  [the longest x2 6.09 us: padded_2(): after = lax.ppermute(leading, axis, down)]
    slice x6 -> x0, local copies, waits for them, and re-layouts: 5.21 us -> none  [the longest x1 4.25 us: local(): along_lon = jnp.concatenate([wind[..., :levels], wind[..., :levels]], -1)]
    unnamed x16 -> x12, local copies, waits for them, and re-layouts: 2.86 us -> 7.23 us
  transfers between devices with their start and end apart: 4 -> 0, of which waited for: 2 -> 0; matrix products, arithmetic and copies ran while one was open for 8% -> 0% of each run, Pallas kernels for 0% -> 0%
where the time goes in v1:
time: 38.4 us; the launch traced here: 38 us
  Pallas kernels  30.8 us (80%)
  local copies, waits for them, and re-layouts  7.23 us (19%)
    pallas_call x1, Pallas kernels, local(): pl.pallas_call(closure_kernel, out_shape=jax.ShapeDtypeStruct((cols, ch),...  21 us
    pallas_call x1, Pallas kernels, local(): pl.pallas_call(functools.partial(advance_kernel, ntx, nty), out_shape=jax...  9.78 us
    unnamed x12, local copies, waits for them, and re-layouts  7.23 us

profile of v1, /device:TPU:0, one launch (start us, length us, event | category | flops | bytes accessed | tf_op | source)
XLA Modules:
  0.0 38.0 jit_solution(2137558044607304176)
XLA Ops:
  0.0 0.8 %copy.8.diffusion_ref = f32[128,32]{1,0:T(8,128)S(1)} copy(f32[128,32]{0,1:T(8,128)} %param.9) | data formatting | bytes 32768 | tf_op args[2]
  0.8 0.8 %copy.9.mask_ref = s32[128,32]{1,0:T(8,128)S(1)} copy(s32[128,32]{0,1:T(8,128)} %param.10) | data formatting | bytes 32768 | tf_op args[3]
  1.6 0.0 copy-start.1
  1.6 1.6 %copy-done.1 = f32[128,32,128]{2,1,0:T(8,128)S(1)} copy-done((f32[128,32,128]{2,1,0:T(8,128)S(1)}, f32[128,32,128]{2,1,0:T(8,128)}, u32[]{:S(2)}) %copy-start.1) | copy-done | bytes 2097176
  3.2 0.0 copy-start.2
  3.2 1.2 %copy-done.2 = bf16[128,32,128]{2,1,0:T(8,128)(2,1)S(1)} copy-done((bf16[128,32,128]{2,1,0:T(8,128)(2,1)S(1)}, bf16[128,32,128]{2,1,0:T(8,128)(2,1)}, u32[]{:S(2)}) %copy-start.2) | copy-done | bytes 1048600
  4.5 0.0 copy-start.3
  4.5 0.0 copy-start.4
  4.5 9.8 %advance.1.adv_hbm = f32[4096,128]{1,0:T(8,128)S(1)} custom-call(f32[128,32,128]{2,1,0:T(8,128)S(1)} %copy-done.1, bf16[128,32,128]{2,1,0:T(8,128)(2,1)S(1)} %copy-done.2, f32[128,32]{1,0:T(8,128)S(1)} %copy.8.diffusion_ref), custom_call_target="tpu_custom_call" | custom-call | tf_op jit(solution)/shard_map/advance/pallas_call | solution.py:206
  14.2 0.0 copy-done.3
  14.3 0.0 copy-done.4
  14.3 0.0 copy-start
  14.3 2.8 %copy-done = bf16[3,1024,1024]{2,1,0:T(8,128)(2,1)S(1)} copy-done((bf16[3,1024,1024]{2,1,0:T(8,128)(2,1)S(1)}, bf16[3,1024,1024]{2,1,0:T(8,128)(2,1)}, u32[]{:S(2)}) %copy-start) | copy-done | bytes 6291480
  17.1 21.0 %closure.1 = f32[4096,128]{1,0:T(8,128)} custom-call(s32[128,32]{1,0:T(8,128)S(1)} %copy.9.mask_ref, f32[4096,128]{1,0:T(8,128)S(1)} %advance.1.adv_hbm, bf16[128,1024]{1,0:T(8,128)(2,1)S(1)} %copy-done.3, bf16[3,1024,1024]{2,1,0:T(8,128)(2,1)S(1)} %copy-done, bf16[1024,128]{1,0:T(8,128)(2,1)S(1)} %copy-done.4), custom_call_target="tpu_custom_call" | custom-call | tf_op jit(solution)/shard_map/closure/pallas_call | solution.py:221
Async XLA Ops:
  1.6 1.6 %copy-start.1 = (f32[128,32,128]{2,1,0:T(8,128)S(1)}, f32[128,32,128]{2,1,0:T(8,128)}, u32[]{:S(2)}) copy-start(f32[128,32,128]{2,1,0:T(8,128)} %state_hbm.1) | copy-start | bytes 6291460
  3.2 1.2 %copy-start.2 = (bf16[128,32,128]{2,1,0:T(8,128)(2,1)S(1)}, bf16[128,32,128]{2,1,0:T(8,128)(2,1)}, u32[]{:S(2)}) copy-start(bf16[128,32,128]{2,1,0:T(8,128)(2,1)} %courant_ref.1) | copy-start | bytes 3145732
  4.5 9.8 %copy-start.3 = (bf16[128,1024]{1,0:T(8,128)(2,1)S(1)}, bf16[128,1024]{1,0:T(8,128)(2,1)}, u32[]{:S(2)}) copy-start(bf16[128,1024]{1,0:T(8,128)(2,1)} %win_hbm.1) | copy-start | bytes 786436
  4.5 9.8 %copy-start.4 = (bf16[1024,128]{1,0:T(8,128)(2,1)S(1)}, bf16[1024,128]{1,0:T(8,128)(2,1)}, u32[]{:S(2)}) copy-start(bf16[1024,128]{1,0:T(8,128)(2,1)} %wout_hbm.1) | copy-start | bytes 786436
  14.3 2.8 %copy-start = (bf16[3,1024,1024]{2,1,0:T(8,128)(2,1)S(1)}, bf16[3,1024,1024]{2,1,0:T(8,128)(2,1)}, u32[]{:S(2)}) copy-start(bf16[3,1024,1024]{2,1,0:T(8,128)(2,1)} %whid_hbm.1) | copy-start | bytes 18874372

commit v2 on v1

v2 whole, which is shorter than its diff:
```python
import functools

import jax
import jax.numpy as jnp
from jax import lax
from jax.experimental import pallas as pl
from jax.experimental.pallas import tpu as pltpu
from jax.sharding import PartitionSpec as P

MESH = pl.DeviceIdType.MESH
PAD = 8
PIECES = 4
GRP = 8
ROOM = (61 << 20) + (3 << 18)
TM = 1024


def advance_kernel(ntx, nty, state_hbm, courant_hbm, diffusion_ref, adv_ref, tile, wind_v, halo_n, halo_s,
                   halo_e, halo_w, coef_n, coef_s, lsem, csem, ssem, rsem):
    lon, lat, ch = wind_v.shape
    ix, iy = lax.axis_index("tx"), lax.axis_index("ty")
    east, west = lax.rem(ix + 1, ntx), lax.rem(ix + ntx - 1, ntx)
    has_n, has_s = iy < nty - 1, iy > 0
    part = lon // PIECES

    barrier = pltpu.get_barrier_semaphore()
    pl.semaphore_signal(barrier, inc=1, device_id={"tx": east}, device_id_type=MESH)
    pl.semaphore_signal(barrier, inc=1, device_id={"tx": west}, device_id_type=MESH)

    @pl.when(has_n)
    def _():
        pl.semaphore_signal(barrier, inc=1, device_id={"ty": iy + 1}, device_id_type=MESH)

    @pl.when(has_s)
    def _():
        pl.semaphore_signal(barrier, inc=1, device_id={"ty": iy - 1}, device_id_type=MESH)

    loads = []
    for k in range(PIECES):
        loads.append((
            pltpu.make_async_copy(state_hbm.at[pl.ds(k * part, part)],
                                  tile.at[pl.ds(1 + k * part, part), pl.ds(PAD, lat)], lsem.at[k]),
            pltpu.make_async_copy(courant_hbm.at[pl.ds(k * part, part)],
                                  wind_v.at[pl.ds(k * part, part)], csem.at[k])))
        for cp in loads[-1]:
            cp.start()

    @pl.when(jnp.logical_not(has_n))
    def _():
        halo_n[...] = jnp.zeros_like(halo_n)

    @pl.when(jnp.logical_not(has_s))
    def _():
        halo_s[...] = jnp.zeros_like(halo_s)

    edge = jnp.zeros((lon, 1, ch), jnp.float32)
    tile[pl.ds(1, lon), pl.ds(PAD - 1, 1), :] = edge
    tile[pl.ds(1, lon), pl.ds(PAD + lat, 1), :] = edge
    tile[pl.ds(0, 1), pl.ds(PAD, lat), :] = jnp.zeros((1, lat, ch), jnp.float32)
    tile[pl.ds(lon + 1, 1), pl.ds(PAD, lat), :] = jnp.zeros((1, lat, ch), jnp.float32)

    pl.semaphore_wait(barrier, 2 + has_n.astype(jnp.int32) + has_s.astype(jnp.int32))

    def send(src, dst, k, dev):
        return pltpu.make_async_remote_copy(
            src_ref=src, dst_ref=dst, send_sem=ssem.at[k], recv_sem=rsem.at[k],
            device_id=dev, device_id_type=MESH)

    to_n = send(state_hbm.at[:, pl.ds(lat - 1, 1)], halo_s, 2, {"ty": iy + 1})
    to_s = send(state_hbm.at[:, pl.ds(0, 1)], halo_n, 3, {"ty": iy - 1})
    to_e = send(state_hbm.at[pl.ds(lon - 1, 1)], halo_w, 0, {"tx": east})
    to_w = send(state_hbm.at[pl.ds(0, 1)], halo_e, 1, {"tx": west})
    pl.when(has_n)(to_n.start)
    pl.when(has_s)(to_s.start)
    to_e.start()
    to_w.start()

    half = ch // 2
    shape = (GRP, lat, ch)
    lane2 = lax.broadcasted_iota(jnp.int32, (GRP * lat, ch), 1)
    lane3 = lax.broadcasted_iota(jnp.int32, shape, 2)
    row3 = lax.broadcasted_iota(jnp.int32, shape, 0)

    def fields(i0):
        wind = wind_v[pl.ds(i0, GRP)].reshape(GRP * lat, ch).astype(jnp.float32) * 0.5
        turned = pltpu.roll(wind, half, 1)
        cx = jnp.where(lane2 < half, wind, turned).reshape(shape)
        cy = jnp.where(lane2 < half, turned, wind).reshape(shape)
        pick = jnp.where(lane3 == row3 + i0, diffusion_ref[...][None], 0.0)
        return cx, cy, jnp.sum(pick, axis=-1, keepdims=True)

    for k in range(PIECES):
        for piece in ([0, 1] if k == 0 else [k + 1]):
            if piece < PIECES:
                for cp in loads[piece]:
                    cp.wait()

        @pl.loop(k * part // GRP, (k + 1) * part // GRP)
        def _(c):
            i0 = pl.multiple_of(c * GRP, GRP)

            def get(di, dj):
                return tile[pl.ds(i0 + 1 + di, GRP), pl.ds(PAD + dj, lat), :]

            mid, e, w, n, s = get(0, 0), get(1, 0), get(-1, 0), get(0, 1), get(0, -1)
            cx, cy, dif = fields(i0)
            coef_n[pl.ds(i0, GRP)] = (dif - cy)[:, lat - 8:]
            coef_s[pl.ds(i0, GRP)] = (dif + cy)[:, :8]
            laplace = e + w + n + s - 4.0 * mid
            adv_ref[pl.ds(i0, GRP)] = mid - cx * (e - w) - cy * (n - s) + dif * laplace

    to_e.wait()
    to_w.wait()

    @pl.when(has_n)
    def _():
        to_n.wait_send()
        to_s.wait_recv()

    @pl.when(has_s)
    def _():
        to_s.wait_send()
        to_n.wait_recv()

    cx, _, dif = fields(0)
    adv_ref[pl.ds(0, 1)] = adv_ref[pl.ds(0, 1)] + ((dif + cx)[:1]) * halo_w[...]
    cx, _, dif = fields(lon - GRP)
    adv_ref[pl.ds(lon - 1, 1)] = adv_ref[pl.ds(lon - 1, 1)] + ((dif - cx)[GRP - 1:]) * halo_e[...]
    sub = lax.broadcasted_iota(jnp.int32, (2 * GRP, 8, ch), 1)

    @pl.loop(0, lon // (2 * GRP))
    def _(c):
        r = pl.ds(pl.multiple_of(c * 2 * GRP, 2 * GRP), 2 * GRP)
        lo, hi = pl.ds(0, 8), pl.ds(lat - 8, 8)
        adv_ref[r, lo, :] = adv_ref[r, lo, :] + jnp.where(sub == 0, coef_s[r] * halo_s[r], 0.0)
        adv_ref[r, hi, :] = adv_ref[r, hi, :] + jnp.where(sub == 7, coef_n[r] * halo_n[r], 0.0)


def closure_kernel(mask_ref, adv, win_hbm, whid_hbm, wout_hbm, out_hbm,
                   done, win, whid, wout, packed, ha, hb, place, base_v, base_s, sems, osem):
    lat, lon = mask_ref.shape
    cols, ch = done.shape
    wide = GRP * lat
    chunks = cols // wide
    span = wide + 16
    layers = whid.shape[0]
    cp_in = pltpu.make_async_copy(win_hbm, win, sems.at[1])
    cp_out = pltpu.make_async_copy(wout_hbm, wout, sems.at[2])
    cp_hid = [pltpu.make_async_copy(whid_hbm.at[l], whid.at[l], sems.at[3 + l]) for l in range(layers)]
    cp_in.start()
    for cp in cp_hid:
        cp.start()
    cp_out.start()

    flags = mask_ref[...].astype(jnp.float32).astype(jnp.bfloat16)
    spread = (lax.broadcasted_iota(jnp.int32, (lat, wide), 1) % lat
              == lax.broadcasted_iota(jnp.int32, (lat, wide), 0)).astype(jnp.float32).astype(jnp.bfloat16)
    rep = lax.dot_general(flags, spread, (((0,), (0,)), ((), ())), preferred_element_type=jnp.float32)
    keep = (lax.broadcasted_iota(jnp.int32, (lon, wide), 1) // lat
            == lax.broadcasted_iota(jnp.int32, (lon, wide), 0) % GRP)
    rows = jnp.sum(jnp.where(keep, rep, 0.0).reshape(chunks, GRP, wide), axis=1)
    upper = (lax.broadcasted_iota(jnp.int32, (wide, wide), 0)
             < lax.broadcasted_iota(jnp.int32, (wide, wide), 1)).astype(jnp.float32).astype(jnp.bfloat16)
    rank = jnp.dot(rows.astype(jnp.bfloat16), upper, preferred_element_type=jnp.float32)
    total = jnp.sum(rows, axis=1, keepdims=True)
    lower = (lax.broadcasted_iota(jnp.int32, (chunks, chunks), 1)
             < lax.broadcasted_iota(jnp.int32, (chunks, chunks), 0)).astype(jnp.float32).astype(jnp.bfloat16)
    base = jnp.dot(lower, jnp.broadcast_to(total, (chunks, 128)).astype(jnp.bfloat16),
                   preferred_element_type=jnp.float32)
    base_i = base.astype(jnp.int32)
    base_v[...] = base_i
    cp_base = pltpu.make_async_copy(base_v, base_s, sems.at[3 + layers])
    cp_base.start()
    rest = (base_i - (base_i // 16) * 16)[:, :1].astype(jnp.float32)
    place[...] = jnp.where(rows > 0.5, rank + rest, -1.0)
    packed[...] = jnp.zeros_like(packed)
    cp_base.wait()

    sub = lax.broadcasted_iota(jnp.int32, (span, wide), 0).astype(jnp.float32)

    def onehot(c):
        row = place[pl.ds(c, 1), :]
        return jnp.where(sub == row, 1.0, 0.0).astype(jnp.bfloat16)

    def start_of(c):
        return pl.multiple_of((base_s[c, 0] // 16) * 16, 16)

    for c in range(chunks):
        b = start_of(c)
        feats = adv[pl.ds(c * GRP, GRP)].reshape(wide, ch).astype(jnp.bfloat16)
        res = jnp.dot(onehot(c), feats, preferred_element_type=jnp.float32).astype(jnp.bfloat16)
        packed[pl.ds(b, 16), :] = packed[pl.ds(b, 16), :] + res[:16]
        packed[pl.ds(pl.multiple_of(b + 16, 16), wide), :] = res[16:]

    cp_in.wait()

    def silu(v):
        hv = 0.5 * v
        return (hv + hv * jnp.tanh(hv)).astype(jnp.bfloat16)

    hid = win.shape[1]
    step = 256

    @pl.loop(0, cols // 2 // TM)
    def _(t):
        r = pl.ds(pl.multiple_of(t * TM, TM), TM)
        x = packed[r, :]
        for n in range(0, hid, step):
            ha[:, n:n + step] = silu(jnp.dot(x, win[:, n:n + step], preferred_element_type=jnp.float32))
        src, dst = ha, hb
        for l in range(layers):
            pl.when(t == 0)(cp_hid[l].wait)
            for n in range(0, hid, step):
                dst[:, n:n + step] = silu(
                    jnp.dot(src[...], whid[l, :, n:n + step], preferred_element_type=jnp.float32))
            src, dst = dst, src
        pl.when(t == 0)(cp_out.wait)
        packed[r, :] = jnp.dot(src[...], wout[...], preferred_element_type=jnp.float32).astype(jnp.bfloat16)

    outs = []
    for c in range(chunks):
        b = start_of(c)
        got = lax.dot_general(onehot(c), packed[pl.ds(b, span), :], (((0,), (0,)), ((), ())),
                              preferred_element_type=jnp.float32)
        r = pl.ds(c * wide, wide)
        done[r, :] = adv[pl.ds(c * GRP, GRP)].reshape(wide, ch) + got
        cp = pltpu.make_async_copy(done.at[r, :], out_hbm.at[r, :], osem.at[c])
        cp.start()
        outs.append(cp)
    for cp in outs:
        cp.wait()


def local(ntx, nty, state, courant, diffusion, conv_mask, w_in, w_hidden, w_out):
    lon, lat, ch = state.shape
    cols = lon * lat
    hid = w_in.shape[1]
    layers = w_hidden.shape[0]
    wide = GRP * lat
    chunks = cols // wide
    vmem = pl.BlockSpec(memory_space=pltpu.VMEM)
    hbm = pl.BlockSpec(memory_space=pltpu.MemorySpace.HBM)
    adv = pl.pallas_call(
        functools.partial(advance_kernel, ntx, nty),
        out_shape=jax.ShapeDtypeStruct((lon, lat, ch), jnp.float32),
        in_specs=[hbm, hbm, vmem],
        out_specs=vmem,
        scratch_shapes=[
            pltpu.VMEM((lon + 2, lat + 2 * PAD, ch), jnp.float32),
            pltpu.VMEM((lon, lat, ch), jnp.bfloat16),
            pltpu.VMEM((lon, 1, ch), jnp.float32),
            pltpu.VMEM((lon, 1, ch), jnp.float32),
            pltpu.VMEM((1, lat, ch), jnp.float32),
            pltpu.VMEM((1, lat, ch), jnp.float32),
            pltpu.VMEM((lon, 8, ch), jnp.float32),
            pltpu.VMEM((lon, 8, ch), jnp.float32),
            pltpu.SemaphoreType.DMA((PIECES,)),
            pltpu.SemaphoreType.DMA((PIECES,)),
            pltpu.SemaphoreType.DMA((4,)),
            pltpu.SemaphoreType.DMA((4,)),
        ],
        compiler_params=pltpu.CompilerParams(collective_id=0, has_side_effects=True,
                                             vmem_limit_bytes=ROOM),
        name="advance",
    )(state, courant, diffusion.T)
    out = pl.pallas_call(
        closure_kernel,
        out_shape=jax.ShapeDtypeStruct((cols, ch), jnp.float32),
        in_specs=[vmem, vmem, hbm, hbm, hbm],
        out_specs=hbm,
        scratch_shapes=[
            pltpu.VMEM((cols, ch), jnp.float32),
            pltpu.VMEM(w_in.shape, jnp.bfloat16),
            pltpu.VMEM(w_hidden.shape, jnp.bfloat16),
            pltpu.VMEM(w_out.shape, jnp.bfloat16),
            pltpu.VMEM((cols // 2 + wide + 32, ch), jnp.bfloat16),
            pltpu.VMEM((TM, hid), jnp.bfloat16),
            pltpu.VMEM((TM, hid), jnp.bfloat16),
            pltpu.VMEM((chunks, wide), jnp.float32),
            pltpu.VMEM((chunks, 128), jnp.int32),
            pltpu.SMEM((chunks, 128), jnp.int32),
            pltpu.SemaphoreType.DMA((4 + layers,)),
            pltpu.SemaphoreType.DMA((chunks,)),
        ],
        compiler_params=pltpu.CompilerParams(vmem_limit_bytes=ROOM),
        name="closure",
    )(conv_mask.T, adv, w_in, w_hidden, w_out)
    return out.reshape(lon, lat, ch)


def solution(mesh):
    spec = P(("member", "tx"), "ty", None)
    flat = P(("member", "tx"), "ty")
    return jax.shard_map(
        functools.partial(local, mesh.shape["tx"], mesh.shape["ty"]),
        mesh=mesh,
        in_specs=(spec, spec, flat, flat, P(), P(), P()),
        out_specs=spec,
        check_vma=False,
    )
```

time: 38.4 us -> 36.3 us (0.945)
  local copies, waits for them, and re-layouts: 7.23 us -> 0 us
  Pallas kernels: 30.8 us -> 36 us
    unnamed x12 -> x0, local copies, waits for them, and re-layouts: 7.23 us -> none
    pallas_call x1, Pallas kernels: 21 us -> 26.3 us  [local(): pl.pallas_call(closure_kernel, out_shape=jax.ShapeDtypeStruct((cols, ch),...]
where the time goes in v2:
time: 36.3 us; the launch traced here: 36 us
  Pallas kernels  36 us (99%)
    pallas_call x1, Pallas kernels, local(): pl.pallas_call(closure_kernel, out_shape=jax.ShapeDtypeStruct((cols, ch),...  26.3 us
    pallas_call x1, Pallas kernels, local(): pl.pallas_call(functools.partial(advance_kernel, ntx, nty), out_shape=jax...  9.68 us

profile of v2, /device:TPU:0, one launch (start us, length us, event | category | flops | bytes accessed | tf_op | source)
XLA Modules:
  0.0 36.0 jit_solution(11669802176992499026)
XLA Ops:
  0.0 9.7 %advance.1.adv = f32[128,32,128]{2,1,0:T(8,128)} custom-call(f32[128,32,128]{2,1,0:T(8,128)} %state_hbm.1, bf16[128,32,128]{2,1,0:T(8,128)(2,1)} %courant_hbm.1, f32[32,128]{1,0:T(8,128)} %bitcast.3), custom_call_target="tpu_custom_call" | custom-call | tf_op jit(solution)/shard_map/advance/pallas_call | solution.py:243
  9.7 26.3 %closure.1 = f32[4096,128]{1,0:T(8,128)} custom-call(s32[32,128]{1,0:T(8,128)} %bitcast.4, f32[128,32,128]{2,1,0:T(8,128)} %advance.1.adv, bf16[128,1024]{1,0:T(8,128)(2,1)} %win_hbm.1, bf16[3,1024,1024]{2,1,0:T(8,128)(2,1)} %whid_hbm.1, bf16[1024,128]{1,0:T(8,128)(2,1)} %wout_hbm.1), custom_call_target="tpu_custom_call" | custom-call | tf_op jit(solution)/shard_map/closure/pallas_call | solution.py:266

commit v3 on v2

--- a/solution.py
+++ b/solution.py
@@ -11,12 +11,13 @@
 PAD = 8
 PIECES = 4
 GRP = 8
-ROOM = (61 << 20) + (3 << 18)
+ROOM = 55 << 20
 TM = 1024
 
 
-def advance_kernel(ntx, nty, state_hbm, courant_hbm, diffusion_ref, adv_ref, tile, wind_v, halo_n, halo_s,
-                   halo_e, halo_w, coef_n, coef_s, lsem, csem, ssem, rsem):
+def advance_kernel(ntx, nty, state_hbm, courant_hbm, diffusion_ref, win_hbm, whid_hbm, wout_hbm,
+                   adv_ref, win_ref, whid_ref, wout_ref, tile, wind_v, halo_n, halo_s,
+                   halo_e, halo_w, coef_n, coef_s, lsem, csem, wsem, ssem, rsem):
     lon, lat, ch = wind_v.shape
     ix, iy = lax.axis_index("tx"), lax.axis_index("ty")
     east, west = lax.rem(ix + 1, ntx), lax.rem(ix + ntx - 1, ntx)
@@ -44,6 +45,10 @@
                                   wind_v.at[pl.ds(k * part, part)], csem.at[k])))
         for cp in loads[-1]:
             cp.start()
+    weights = [pltpu.make_async_copy(src, dst, wsem.at[k]) for k, (src, dst) in enumerate(
+        ((win_hbm, win_ref), (whid_hbm, whid_ref), (wout_hbm, wout_ref)))]
+    for cp in weights:
+        cp.start()
 
     @pl.when(jnp.logical_not(has_n))
     def _():
@@ -135,23 +140,17 @@
         adv_ref[r, lo, :] = adv_ref[r, lo, :] + jnp.where(sub == 0, coef_s[r] * halo_s[r], 0.0)
         adv_ref[r, hi, :] = adv_ref[r, hi, :] + jnp.where(sub == 7, coef_n[r] * halo_n[r], 0.0)
 
-
-def closure_kernel(mask_ref, adv, win_hbm, whid_hbm, wout_hbm, out_hbm,
-                   done, win, whid, wout, packed, ha, hb, place, base_v, base_s, sems, osem):
+    for cp in weights:
+        cp.wait()
+
+
+def closure_kernel(mask_ref, adv, win, whid, wout, out_hbm, done, packed, ha, hb, place, base_v, base_s, bsem, osem):
     lat, lon = mask_ref.shape
     cols, ch = done.shape
     wide = GRP * lat
     chunks = cols // wide
     span = wide + 16
     layers = whid.shape[0]
-    cp_in = pltpu.make_async_copy(win_hbm, win, sems.at[1])
-    cp_out = pltpu.make_async_copy(wout_hbm, wout, sems.at[2])
-    cp_hid = [pltpu.make_async_copy(whid_hbm.at[l], whid.at[l], sems.at[3 + l]) for l in range(layers)]
-    cp_in.start()
-    for cp in cp_hid:
-        cp.start()
-    cp_out.start()
-
     flags = mask_ref[...].astype(jnp.float32).astype(jnp.bfloat16)
     spread = (lax.broadcasted_iota(jnp.int32, (lat, wide), 1) % lat
               == lax.broadcasted_iota(jnp.int32, (lat, wide), 0)).astype(jnp.float32).astype(jnp.bfloat16)
@@ -169,7 +168,7 @@
                    preferred_element_type=jnp.float32)
     base_i = base.astype(jnp.int32)
     base_v[...] = base_i
-    cp_base = pltpu.make_async_copy(base_v, base_s, sems.at[3 + layers])
+    cp_base = pltpu.make_async_copy(base_v, base_s, bsem)
     cp_base.start()
     rest = (base_i - (base_i // 16) * 16)[:, :1].astype(jnp.float32)
     place[...] = jnp.where(rows > 0.5, rank + rest, -1.0)
@@ -191,8 +190,6 @@
         res = jnp.dot(onehot(c), feats, preferred_element_type=jnp.float32).astype(jnp.bfloat16)
         packed[pl.ds(b, 16), :] = packed[pl.ds(b, 16), :] + res[:16]
         packed[pl.ds(pl.multiple_of(b + 16, 16), wide), :] = res[16:]
-
-    cp_in.wait()
 
     def silu(v):
         hv = 0.5 * v
@@ -209,12 +206,10 @@
             ha[:, n:n + step] = silu(jnp.dot(x, win[:, n:n + step], preferred_element_type=jnp.float32))
         src, dst = ha, hb
         for l in range(layers):
-            pl.when(t == 0)(cp_hid[l].wait)
             for n in range(0, hid, step):
                 dst[:, n:n + step] = silu(
                     jnp.dot(src[...], whid[l, :, n:n + step], preferred_element_type=jnp.float32))
             src, dst = dst, src
-        pl.when(t == 0)(cp_out.wait)
         packed[r, :] = jnp.dot(src[...], wout[...], preferred_element_type=jnp.float32).astype(jnp.bfloat16)
 
     outs = []
@@ -235,16 +230,20 @@
     lon, lat, ch = state.shape
     cols = lon * lat
     hid = w_in.shape[1]
-    layers = w_hidden.shape[0]
     wide = GRP * lat
     chunks = cols // wide
     vmem = pl.BlockSpec(memory_space=pltpu.VMEM)
     hbm = pl.BlockSpec(memory_space=pltpu.MemorySpace.HBM)
-    adv = pl.pallas_call(
+    adv, w_in, w_hidden, w_out = pl.pallas_call(
         functools.partial(advance_kernel, ntx, nty),
-        out_shape=jax.ShapeDtypeStruct((lon, lat, ch), jnp.float32),
-        in_specs=[hbm, hbm, vmem],
-        out_specs=vmem,
+        out_shape=[
+            pltpu.VMEM((lon, lat, ch), jnp.float32),
+            pltpu.VMEM(w_in.shape, jnp.bfloat16),
+            pltpu.VMEM(w_hidden.shape, jnp.bfloat16),
+            pltpu.VMEM(w_out.shape, jnp.bfloat16),
+        ],
+        in_specs=[hbm, hbm, vmem, hbm, hbm, hbm],
+        out_specs=[vmem] * 4,
         scratch_shapes=[
             pltpu.VMEM((lon + 2, lat + 2 * PAD, ch), jnp.float32),
             pltpu.VMEM((lon, lat, ch), jnp.bfloat16),
@@ -256,33 +255,31 @@
             pltpu.VMEM((lon, 8, ch), jnp.float32),
             pltpu.SemaphoreType.DMA((PIECES,)),
             pltpu.SemaphoreType.DMA((PIECES,)),
+            pltpu.SemaphoreType.DMA((3,)),
             pltpu.SemaphoreType.DMA((4,)),
             pltpu.SemaphoreType.DMA((4,)),
         ],
         compiler_params=pltpu.CompilerParams(collective_id=0, has_side_effects=True,
                                              vmem_limit_bytes=ROOM),
         name="advance",
-    )(state, courant, diffusion.T)
+    )(state, courant, diffusion.T, w_in, w_hidden, w_out)
     out = pl.pallas_call(
         closure_kernel,
         out_shape=jax.ShapeDtypeStruct((cols, ch), jnp.float32),
-        in_specs=[vmem, vmem, hbm, hbm, hbm],
+        in_specs=[vmem] * 5,
         out_specs=hbm,
         scratch_shapes=[
             pltpu.VMEM((cols, ch), jnp.float32),
-            pltpu.VMEM(w_in.shape, jnp.bfloat16),
-            pltpu.VMEM(w_hidden.shape, jnp.bfloat16),
-            pltpu.VMEM(w_out.shape, jnp.bfloat16),
             pltpu.VMEM((cols // 2 + wide + 32, ch), jnp.bfloat16),
             pltpu.VMEM((TM, hid), jnp.bfloat16),
             pltpu.VMEM((TM, hid), jnp.bfloat16),
             pltpu.VMEM((chunks, wide), jnp.float32),
             pltpu.VMEM((chunks, 128), jnp.int32),
             pltpu.SMEM((chunks, 128), jnp.int32),
-            pltpu.SemaphoreType.DMA((4 + layers,)),
+            pltpu.SemaphoreType.DMA,
             pltpu.SemaphoreType.DMA((chunks,)),
         ],
-        compiler_params=pltpu.CompilerParams(vmem_limit_bytes=ROOM),
+        compiler_params=pltpu.CompilerParams(vmem_limit_bytes=ROOM // 2),
         name="closure",
     )(conv_mask.T, adv, w_in, w_hidden, w_out)
     return out.reshape(lon, lat, ch)

time: 36.3 us -> 28.5 us (0.79)
  Pallas kernels: 36 us -> 28.2 us
    pallas_call x1, Pallas kernels: 26.3 us -> 19.9 us  [local(): pl.pallas_call(closure_kernel, out_shape=jax.ShapeDtypeStruct((cols, ch),...]
    pallas_call x1, Pallas kernels: 9.68 us -> 8.38 us  [local(): pl.pallas_call(functools.partial(advance_kernel, ntx, nty), out_shape=[pl...]
where the time goes in v3:
time: 28.5 us; the launch traced here: 28.3 us
  Pallas kernels  28.2 us (99%)
    pallas_call x1, Pallas kernels, local(): pl.pallas_call(closure_kernel, out_shape=jax.ShapeDtypeStruct((cols, ch),...  19.9 us
    pallas_call x1, Pallas kernels, local(): pl.pallas_call(functools.partial(advance_kernel, ntx, nty), out_shape=[pl...  8.38 us

profile of v3, /device:TPU:0, one launch (start us, length us, event | category | flops | bytes accessed | tf_op | source)
XLA Modules:
  0.0 28.3 jit_solution(17522020113475205427)
XLA Ops:
  0.0 0.0 copy-start
  0.0 8.4 %advance.1 = (f32[128,32,128]{2,1,0:T(8,128)S(1)}, bf16[128,1024]{1,0:T(8,128)(2,1)S(1)}, bf16[3,1024,1024]{2,1,0:T(8,128)(2,1)S(1)}, bf16[1024,128]{1,0:T(8,128)(2,1)S(1)}) custom-call(f32[128,32,128]{2,1,0:T(8,128)} %state_hbm.1, bf16[128,32,128]{2,1,0:T(8,128)(2,1)} %courant_hbm.1, f32[32,128]{1,0:T(8,128)} %bitcast.4, bf16[128,1024]{1,0:T(8,128)(2,1)} %win_hbm.1, ...), custom_call_target="tpu_custom_call" | custom-call | tf_op jit(solution)/shard_map/advance/pallas_call | solution.py:237
  8.4 0.0 copy-done
  8.4 19.9 %closure.1 = f32[4096,128]{1,0:T(8,128)} custom-call(s32[32,128]{1,0:T(8,128)S(1)} %bitcast.3, f32[128,32,128]{2,1,0:T(8,128)S(1)} %get-tuple-element.9.adv, bf16[128,1024]{1,0:T(8,128)(2,1)S(1)} %get-tuple-element.10.win, bf16[3,1024,1024]{2,1,0:T(8,128)(2,1)S(1)} %get-tuple-element.11.whid, bf16[1024,128]{1,0:T(8,128)(2,1)S(1)} %get-tuple-element.12.wout), custom_call_target="tpu_custom_call" | custom-call | tf_op jit(solution)/shard_map/closure/pallas_call | solution.py:266
Async XLA Ops:
  0.0 8.4 %copy-start = (s32[128,32]{0,1:T(8,128)S(1)}, s32[128,32]{0,1:T(8,128)}, u32[]{:S(2)}) copy-start(s32[128,32]{0,1:T(8,128)} %param.10) | copy-start | bytes 49156
